TPU v7x, 128 devices: a whole 4x4x4 slice. The times are simulated.
128 devices in a mesh: cfg: 2 (over core), req: 4 (over y), seq: 16 (over z, x).
Axes of the slice: x: 4, y: 4, z: 4, core: 2. Of those that a mesh axis runs over, the one named last changes fastest.
Arguments:
- img_qkv: bfloat16 [2, 8, 4096, 6144], P('cfg', 'req', 'seq'), may hold values from -4.5 to 4.5
- txt_kv: bfloat16 [2, 8, 512, 4096], P('cfg', 'req', 'seq'), may hold values from -4.5 to 4.5
- text_len: int32 [8], P('req'), may hold values from 77 to 512
- t_index: int32 [8], P('req'), may hold values from 0 to 3
- guidance: float32 [8], P('req'), may hold values from 1.5 to 6
- modulation: float32 [2, 8, 3, 3072], P('cfg', 'req'), may hold values from -4 to 4
- img_hidden: bfloat16 [2, 8, 4096, 3072], P('cfg', 'req', 'seq'), may hold values from -6 to 6
- latents: float32 [8, 4096, 64], P('req', 'seq', 'cfg'), may hold values from -6 to 6
- proj_weight: bfloat16 [2048, 3072], P(('cfg', 'req', 'seq')), may hold values from -0.125 to 0.125
- final_weight: bfloat16 [3072, 64], replicated, may hold values from -0.109375 to 0.109375
Outputs:
- latents_next: float32 [8, 4096, 64], P('req', 'seq', 'cfg')
- vel_norm: float32 [2, 8], P('cfg', 'req')
- max_logit: float32 [2, 8], P('cfg', 'req')
All inputs are finite; a program needn't handle non-finite values.
Results may differ from a plain program's by a relative error of at most 0.0033.
Values may be sent and summed in bfloat16 or wider, within the bound.
A program may use at most 128 MiB of HBM per device.

v0:
```python
import math
import jax
import jax.numpy as jnp
from jax import lax
from jax.sharding import PartitionSpec as P

HEADS = 16
HD = 128
STEPS = 4
time_shift = 1.15
norm_eps = 1e-06


def swapped(value, axis, stride):
    return lax.ppermute(value, axis, [(i, i ^ 1 << stride) for i in range(lax.axis_size(axis))])


def sigma_of(step_index):
    fraction = 1.0 - step_index.astype(jnp.float32) / STEPS
    lifted = fraction * math.exp(time_shift)
    return lifted / (lifted + 1.0 - fraction)


def shards(
    img_qkv,
    txt_kv,
    text_len,
    t_index,
    guidance,
    modulation,
    img_hidden,
    latents,
    proj_weight,
    final_weight,
):
    local_prompts = img_qkv.shape[1]
    img_dev = img_qkv.shape[2]
    txt_dev = txt_kv.shape[2]
    joined = img_qkv[0].reshape(local_prompts, img_dev, 3, HEADS, HD)
    text_rows = txt_kv[0].reshape(local_prompts, txt_dev, 2, HEADS, HD)
    full_img, full_txt = (
        lax.all_to_all(joined, "seq", split_axis=3, concat_axis=1, tiled=True),
        lax.all_to_all(text_rows, "seq", split_axis=3, concat_axis=1, tiled=True),
    )
    img_len = full_img.shape[1]
    txt_len = full_txt.shape[1]
    local_heads = full_img.shape[3]
    block_rows = math.gcd(img_len, 1024)
    mixed_list = []
    max_list = []
    for prompt in range(local_prompts):
        key_rows = jnp.concatenate([full_txt[prompt, :, 0], full_img[prompt, :, 1]], axis=0)
        value_rows = jnp.concatenate([full_txt[prompt, :, 1], full_img[prompt, :, 2]], axis=0)
        key_valid = jnp.concatenate(
            [jnp.arange(txt_len) < text_len[prompt], jnp.ones((img_len,), jnp.bool_)]
        )

        def one_block(query_rows):
            logits = jnp.einsum(
                "qhd,khd->hqk", query_rows, key_rows, preferred_element_type=jnp.float32
            ) * HD ** (-0.5)
            logits = jnp.where(key_valid[None, None, :], logits, -jnp.inf)
            row_max = jnp.max(logits, axis=2, keepdims=True)
            weights = jnp.exp(logits - row_max)
            weights = (weights / jnp.sum(weights, axis=2, keepdims=True)).astype(jnp.bfloat16)
            mixed_rows = jnp.einsum(
                "hqk,khd->qhd", weights, value_rows, preferred_element_type=jnp.float32
            ).astype(jnp.bfloat16)
            return (mixed_rows, jnp.max(row_max))

        mixed_rows, top_logit = lax.map(
            one_block,
            full_img[prompt, :, 0].reshape(img_len // block_rows, block_rows, local_heads, HD),
        )
        mixed_list.append(mixed_rows.reshape(img_len, local_heads, HD))
        max_list.append(jnp.max(top_logit))
    local_max = jnp.stack(max_list)
    head_rows = jnp.stack(mixed_list)
    token_rows = lax.all_to_all(head_rows, "seq", split_axis=1, concat_axis=2, tiled=True)
    attended = token_rows.reshape(local_prompts * img_dev, HEADS * HD)
    projected = jnp.dot(
        attended,
        lax.all_gather(proj_weight, ("cfg", "req", "seq"), axis=0, tiled=True),
        preferred_element_type=jnp.float32,
    )
    projected = projected.reshape(local_prompts, img_dev, projected.shape[1])
    mod_rows = modulation[0]
    hidden = img_hidden[0].astype(jnp.float32) + mod_rows[:, 0][:, None, :] * projected
    average = jnp.mean(hidden, axis=2, keepdims=True)
    centred = hidden - average
    variance = jnp.mean(centred * centred, axis=2, keepdims=True)
    normed = (
        centred / jnp.sqrt(variance + norm_eps) * (1.0 + mod_rows[:, 1][:, None, :])
        + mod_rows[:, 2][:, None, :]
    ).astype(jnp.bfloat16)
    velocity = jnp.einsum("ptd,dc->ptc", normed, final_weight, preferred_element_type=jnp.float32)
    half_chan = latents.shape[2]
    copy_pos = lax.axis_index("cfg")
    own_part = lax.dynamic_slice_in_dim(velocity, copy_pos * half_chan, half_chan, 2)
    other_part = lax.dynamic_slice_in_dim(velocity, (1 - copy_pos) * half_chan, half_chan, 2)
    partner = swapped(other_part, "cfg", 0)
    is_cond = copy_pos == 0
    cond_vel = jnp.where(is_cond, own_part, partner)
    uncond_vel = jnp.where(is_cond, partner, own_part)
    guided = uncond_vel + guidance[:, None, None] * (cond_vel - uncond_vel)
    square_sum = jnp.sum(guided * guided, axis=(1, 2))
    total_sq = lax.psum(square_sum, "seq")
    global_max = lax.pmax(local_max, "seq")
    vel_norm = jnp.sqrt(total_sq / (img_len * half_chan) + norm_eps)
    euler_step = sigma_of(t_index + 1) - sigma_of(t_index)
    advanced = latents + euler_step[:, None, None] * guided
    return (advanced, vel_norm.reshape(1, local_prompts), global_max.reshape(1, local_prompts))


def solution(mesh):
    return jax.shard_map(
        shards,
        mesh=mesh,
        in_specs=(
            P("cfg", "req", "seq", None),
            P("cfg", "req", "seq", None),
            P("req"),
            P("req"),
            P("req"),
            P("cfg", "req", None, None),
            P("cfg", "req", "seq", None),
            P("req", "seq", "cfg"),
            P(("cfg", "req", "seq"), None),
            P(),
        ),
        out_specs=(P("req", "seq", "cfg"), P("cfg", "req"), P("cfg", "req")),
        check_vma=False,
    )
```

profile of v0, /device:TPU:24, one launch (start us, length us, event | category | flops | bytes accessed | tf_op | source)
XLA Modules:
  0.0 548.9 jit_solution(1137736579929246898)
XLA Ops:
  7.2 1.2 copy.41
  9.4 7.9 %all-to-all-start.1 = ((bf16[2,32,2,16,128]{4,1,2,0,3:T(8,128)(2,1)}), bf16[2,32,2,16,128]{4,1,2,0,3:T(8,128)(2,1)S(1)}, u32[]{:S(2)}, u32[]{:S(2)}) async-start(bf16[2,32,2,16,128]{4,1,2,0,3:T(8,128)(2,1)} %copy.34), calls=%async_computation.1 | async-start | bytes 1048576 | tf_op jit(solution)/shard_map/all_to_all | solution.py:43
  17.3 8.6 %copy.31 = bf16[1,2,256,6144]{2,3,1,0:T(8,128)(2,1)} copy(bf16[1,2,256,6144]{3,2,1,0:T(8,128)(2,1)} %param.14) | data formatting | bytes 12582912 | tf_op args[0]
  25.9 8.7 %copy.32 = bf16[2,256,3,16,128]{4,1,2,0,3:T(8,128)(2,1)} copy(bf16[2,256,3,16,128]{1,4,3,2,0:T(8,128)(2,1)} %bitcast.151) | data formatting | bytes 12582912 | tf_op jit(solution)/shard_map/reshape;squeeze | solution.py:39
  34.6 7.4 %all-to-all-start = ((bf16[2,256,3,16,128]{4,1,2,0,3:T(8,128)(2,1)}), bf16[2,256,3,16,128]{4,1,2,0,3:T(8,128)(2,1)}, u32[]{:S(2)}, u32[]{:S(2)}) async-start(bf16[2,256,3,16,128]{4,1,2,0,3:T(8,128)(2,1)} %copy.32), calls=%async_computation | async-start | bytes 12582912 | tf_op jit(solution)/shard_map/all_to_all | solution.py:42
  46.1 93.6 %all-to-all-done = bf16[2,256,3,16,128]{4,1,2,0,3:T(8,128)(2,1)} async-done(((bf16[2,256,3,16,128]{4,1,2,0,3:T(8,128)(2,1)}), bf16[2,256,3,16,128]{4,1,2,0,3:T(8,128)(2,1)}, u32[]{:S(2)}, u32[]{:S(2)}) %all-to-all-start) | async-done | bytes 6291488 | tf_op jit(solution)/shard_map/all_to_all | solution.py:42
  139.7 3.2 copy.33
  142.9 1.7 slice_bitcast_fusion.2
  144.7 1.2 pad_maximum_fusion.1
  145.9 1.1 broadcast.86.clone.1
  147.0 122.4 %while.24 = (s32[]{:T(128)}, bf16[4,1024,1,128]{3,1,2,0:T(8,128)(2,1)}, f32[4]{0:T(128)S(1)}, pred[4608]{0:T(1024)(128)(4,1)S(1)}, bf16[4,1024,1,128]{3,1,2,0:T(...) while((s32[]{:T(128)}, ...), condition=%wide.region_4.5_spmd, body=%wide.region_0.4_spmd.sunk | while | flops 2477389824 | bytes 59542120 | solution.py:71
  147.0 8.2 %fusion.57 = (f32[1024]{0:T(1024)S(1)}, f32[1024,4608]{1,0:T(8,128)}) fusion(pred[4608]{0:T(1024)(128)(4,1)S(1)} %get-tuple-element.343, bf16[4608,1,128]{2,0,1:T(8,128)(2,1)S(1)} %get-tuple-element.345, bf16[4,1024,1,128]{3,1,2,0:T(8,128)(2,1)S(1)} %get-tuple-element.344, s32[]{:T(128)} %get-tuple-element.332), kind=kOutput, calls=%fused_computation.5.clone.1 | convolution fusion | flops 1222114304 | bytes 20325380 | tf_op jit(solution)/shard_map/while/body/eval_jaxpr/qhd,khd->hqk/dot_general | solution.py:59
  155.2 13.3 %fusion.58 = (f32[]{:T(128)}, f32[1024]{0:T(1024)S(1)}) fusion(f32[1024,4608]{1,0:T(8,128)} %get-tuple-element.285, pred[4608]{0:T(1024)(128)(4,1)S(1)} %get-tuple-element.343, f32[1024]{0:T(1024)S(1)} %get-tuple-element.286), kind=kLoop, calls=%fused_computation.4.clone.1 | loop fusion | flops 23591936 | bytes 18887172 | tf_op jit(solution)/shard_map/while/body/eval_jaxpr/reduce_max | solution.py:69
  168.5 9.6 %fusion.59 = bf16[4,1024,1,128]{3,1,2,0:T(8,128)(2,1)} fusion(bf16[4,1024,1,128]{3,1,2,0:T(8,128)(2,1)} %get-tuple-element.333, s32[]{:T(128)} %get-tuple-element.332, bf16[4608,1,128]{2,0,1:T(8,128)(2,1)} %get-tuple-element.346, f32[1024,4608]{1,0:T(8,128)} %get-tuple-element.285, f32[1024]{0:T(1024)S(1)} %get-tuple-element.287, ...), kind=kOutput, calls=%fused_computation.12.clone.1 | convolution fusion | flops 1231683584 | bytes 20329472 | tf_op jit(solution)/shard_map/while/body/eval_jaxpr/hqk,khd->qhd/dot_general | solution.py:66
  178.8 7.9 %fusion.57 = (f32[1024]{0:T(1024)S(1)}, f32[1024,4608]{1,0:T(8,128)}) fusion(pred[4608]{0:T(1024)(128)(4,1)S(1)} %get-tuple-element.343, bf16[4608,1,128]{2,0,1:T(8,128)(2,1)S(1)} %get-tuple-element.345, bf16[4,1024,1,128]{3,1,2,0:T(8,128)(2,1)S(1)} %get-tuple-element.344, s32[]{:T(128)} %get-tuple-element.332), kind=kOutput, calls=%fused_computation.5.clone.1 | convolution fusion | flops 1222114304 | bytes 20325380 | tf_op jit(solution)/shard_map/while/body/eval_jaxpr/qhd,khd->hqk/dot_general | solution.py:59
  186.7 12.0 %fusion.58 = (f32[]{:T(128)}, f32[1024]{0:T(1024)S(1)}) fusion(f32[1024,4608]{1,0:T(8,128)} %get-tuple-element.285, pred[4608]{0:T(1024)(128)(4,1)S(1)} %get-tuple-element.343, f32[1024]{0:T(1024)S(1)} %get-tuple-element.286), kind=kLoop, calls=%fused_computation.4.clone.1 | loop fusion | flops 23591936 | bytes 18887172 | tf_op jit(solution)/shard_map/while/body/eval_jaxpr/reduce_max | solution.py:69
  198.7 9.6 %fusion.59 = bf16[4,1024,1,128]{3,1,2,0:T(8,128)(2,1)} fusion(bf16[4,1024,1,128]{3,1,2,0:T(8,128)(2,1)} %get-tuple-element.333, s32[]{:T(128)} %get-tuple-element.332, bf16[4608,1,128]{2,0,1:T(8,128)(2,1)} %get-tuple-element.346, f32[1024,4608]{1,0:T(8,128)} %get-tuple-element.285, f32[1024]{0:T(1024)S(1)} %get-tuple-element.287, ...), kind=kOutput, calls=%fused_computation.12.clone.1 | convolution fusion | flops 1231683584 | bytes 20329472 | tf_op jit(solution)/shard_map/while/body/eval_jaxpr/hqk,khd->qhd/dot_general | solution.py:66
  209.0 7.9 %fusion.57 = (f32[1024]{0:T(1024)S(1)}, f32[1024,4608]{1,0:T(8,128)}) fusion(pred[4608]{0:T(1024)(128)(4,1)S(1)} %get-tuple-element.343, bf16[4608,1,128]{2,0,1:T(8,128)(2,1)S(1)} %get-tuple-element.345, bf16[4,1024,1,128]{3,1,2,0:T(8,128)(2,1)S(1)} %get-tuple-element.344, s32[]{:T(128)} %get-tuple-element.332), kind=kOutput, calls=%fused_computation.5.clone.1 | convolution fusion | flops 1222114304 | bytes 20325380 | tf_op jit(solution)/shard_map/while/body/eval_jaxpr/qhd,khd->hqk/dot_general | solution.py:59
  216.9 12.0 %fusion.58 = (f32[]{:T(128)}, f32[1024]{0:T(1024)S(1)}) fusion(f32[1024,4608]{1,0:T(8,128)} %get-tuple-element.285, pred[4608]{0:T(1024)(128)(4,1)S(1)} %get-tuple-element.343, f32[1024]{0:T(1024)S(1)} %get-tuple-element.286), kind=kLoop, calls=%fused_computation.4.clone.1 | loop fusion | flops 23591936 | bytes 18887172 | tf_op jit(solution)/shard_map/while/body/eval_jaxpr/reduce_max | solution.py:69
  228.9 9.6 %fusion.59 = bf16[4,1024,1,128]{3,1,2,0:T(8,128)(2,1)} fusion(bf16[4,1024,1,128]{3,1,2,0:T(8,128)(2,1)} %get-tuple-element.333, s32[]{:T(128)} %get-tuple-element.332, bf16[4608,1,128]{2,0,1:T(8,128)(2,1)} %get-tuple-element.346, f32[1024,4608]{1,0:T(8,128)} %get-tuple-element.285, f32[1024]{0:T(1024)S(1)} %get-tuple-element.287, ...), kind=kOutput, calls=%fused_computation.12.clone.1 | convolution fusion | flops 1231683584 | bytes 20329472 | tf_op jit(solution)/shard_map/while/body/eval_jaxpr/hqk,khd->qhd/dot_general | solution.py:66
  239.2 7.9 %fusion.57 = (f32[1024]{0:T(1024)S(1)}, f32[1024,4608]{1,0:T(8,128)}) fusion(pred[4608]{0:T(1024)(128)(4,1)S(1)} %get-tuple-element.343, bf16[4608,1,128]{2,0,1:T(8,128)(2,1)S(1)} %get-tuple-element.345, bf16[4,1024,1,128]{3,1,2,0:T(8,128)(2,1)S(1)} %get-tuple-element.344, s32[]{:T(128)} %get-tuple-element.332), kind=kOutput, calls=%fused_computation.5.clone.1 | convolution fusion | flops 1222114304 | bytes 20325380 | tf_op jit(solution)/shard_map/while/body/eval_jaxpr/qhd,khd->hqk/dot_general | solution.py:59
  247.1 12.0 %fusion.58 = (f32[]{:T(128)}, f32[1024]{0:T(1024)S(1)}) fusion(f32[1024,4608]{1,0:T(8,128)} %get-tuple-element.285, pred[4608]{0:T(1024)(128)(4,1)S(1)} %get-tuple-element.343, f32[1024]{0:T(1024)S(1)} %get-tuple-element.286), kind=kLoop, calls=%fused_computation.4.clone.1 | loop fusion | flops 23591936 | bytes 18887172 | tf_op jit(solution)/shard_map/while/body/eval_jaxpr/reduce_max | solution.py:69
  259.1 9.6 %fusion.59 = bf16[4,1024,1,128]{3,1,2,0:T(8,128)(2,1)} fusion(bf16[4,1024,1,128]{3,1,2,0:T(8,128)(2,1)} %get-tuple-element.333, s32[]{:T(128)} %get-tuple-element.332, bf16[4608,1,128]{2,0,1:T(8,128)(2,1)} %get-tuple-element.346, f32[1024,4608]{1,0:T(8,128)} %get-tuple-element.285, f32[1024]{0:T(1024)S(1)} %get-tuple-element.287, ...), kind=kOutput, calls=%fused_computation.12.clone.1 | convolution fusion | flops 1231683584 | bytes 20329472 | tf_op jit(solution)/shard_map/while/body/eval_jaxpr/hqk,khd->qhd/dot_general | solution.py:66
  269.4 2.7 pad_maximum_fusion.3
  272.3 122.5 %while.25 = (s32[]{:T(128)}, bf16[4,1024,1,128]{3,1,2,0:T(8,128)(2,1)S(1)}, f32[4]{0:T(128)S(1)}, pred[4608]{0:T(1024)(128)(4,1)S(1)}, bf16[4,1024,1,128]{3,1,2,...) while((s32[]{:T(128)}, ...), condition=%wide.region_9.10_spmd, body=%wide.region_5.9_spmd.sunk | while | flops 2477389824 | bytes 59542120 | solution.py:71
  272.5 8.9 %fusion.61 = (f32[1024]{0:T(1024)S(1)}, f32[1024,4608]{1,0:T(8,128)}) fusion(pred[4608]{0:T(1024)(128)(4,1)S(1)} %get-tuple-element.319, bf16[4608,1,128]{2,0,1:T(8,128)(2,1)S(1)} %get-tuple-element.321, bf16[4,1024,1,128]{3,1,2,0:T(8,128)(2,1)} %get-tuple-element.320, s32[]{:T(128)} %get-tuple-element.308), kind=kOutput, calls=%fused_computation.23.clone.1 | convolution fusion | flops 1222114304 | bytes 20325376 | tf_op jit(solution)/shard_map/while/body/eval_jaxpr/qhd,khd->hqk/dot_general | solution.py:59
  281.3 12.0 %fusion.62 = (f32[]{:T(128)}, f32[1024]{0:T(1024)S(1)}) fusion(f32[1024,4608]{1,0:T(8,128)} %get-tuple-element.296, pred[4608]{0:T(1024)(128)(4,1)S(1)} %get-tuple-element.319, f32[1024]{0:T(1024)S(1)} %get-tuple-element.297), kind=kLoop, calls=%fused_computation.22.clone.1 | loop fusion | flops 23591936 | bytes 18887172 | tf_op jit(solution)/shard_map/while/body/eval_jaxpr/reduce_max | solution.py:69
  293.3 9.0 %fusion.63 = bf16[4,1024,1,128]{3,1,2,0:T(8,128)(2,1)S(1)} fusion(bf16[4,1024,1,128]{3,1,2,0:T(8,128)(2,1)S(1)} %get-tuple-element.309, s32[]{:T(128)} %get-tuple-element.308, bf16[4608,1,128]{2,0,1:T(8,128)(2,1)} %get-tuple-element.322, f32[1024,4608]{1,0:T(8,128)} %get-tuple-element.296, f32[1024]{0:T(1024)S(1)} %get-tuple-element.298, ...), kind=kOutput, calls=%fused_computation.30.clone.1 | convolution fusion | flops 1231683584 | bytes 20329476 | tf_op jit(solution)/shard_map/while/body/eval_jaxpr/hqk,khd->qhd/dot_general | solution.py:66
  303.1 8.8 %fusion.61 = (f32[1024]{0:T(1024)S(1)}, f32[1024,4608]{1,0:T(8,128)}) fusion(pred[4608]{0:T(1024)(128)(4,1)S(1)} %get-tuple-element.319, bf16[4608,1,128]{2,0,1:T(8,128)(2,1)S(1)} %get-tuple-element.321, bf16[4,1024,1,128]{3,1,2,0:T(8,128)(2,1)} %get-tuple-element.320, s32[]{:T(128)} %get-tuple-element.308), kind=kOutput, calls=%fused_computation.23.clone.1 | convolution fusion | flops 1222114304 | bytes 20325376 | tf_op jit(solution)/shard_map/while/body/eval_jaxpr/qhd,khd->hqk/dot_general | solution.py:59
  311.9 12.0 %fusion.62 = (f32[]{:T(128)}, f32[1024]{0:T(1024)S(1)}) fusion(f32[1024,4608]{1,0:T(8,128)} %get-tuple-element.296, pred[4608]{0:T(1024)(128)(4,1)S(1)} %get-tuple-element.319, f32[1024]{0:T(1024)S(1)} %get-tuple-element.297), kind=kLoop, calls=%fused_computation.22.clone.1 | loop fusion | flops 23591936 | bytes 18887172 | tf_op jit(solution)/shard_map/while/body/eval_jaxpr/reduce_max | solution.py:69
  323.9 9.0 %fusion.63 = bf16[4,1024,1,128]{3,1,2,0:T(8,128)(2,1)S(1)} fusion(bf16[4,1024,1,128]{3,1,2,0:T(8,128)(2,1)S(1)} %get-tuple-element.309, s32[]{:T(128)} %get-tuple-element.308, bf16[4608,1,128]{2,0,1:T(8,128)(2,1)} %get-tuple-element.322, f32[1024,4608]{1,0:T(8,128)} %get-tuple-element.296, f32[1024]{0:T(1024)S(1)} %get-tuple-element.298, ...), kind=kOutput, calls=%fused_computation.30.clone.1 | convolution fusion | flops 1231683584 | bytes 20329476 | tf_op jit(solution)/shard_map/while/body/eval_jaxpr/hqk,khd->qhd/dot_general | solution.py:66
  333.6 8.8 %fusion.61 = (f32[1024]{0:T(1024)S(1)}, f32[1024,4608]{1,0:T(8,128)}) fusion(pred[4608]{0:T(1024)(128)(4,1)S(1)} %get-tuple-element.319, bf16[4608,1,128]{2,0,1:T(8,128)(2,1)S(1)} %get-tuple-element.321, bf16[4,1024,1,128]{3,1,2,0:T(8,128)(2,1)} %get-tuple-element.320, s32[]{:T(128)} %get-tuple-element.308), kind=kOutput, calls=%fused_computation.23.clone.1 | convolution fusion | flops 1222114304 | bytes 20325376 | tf_op jit(solution)/shard_map/while/body/eval_jaxpr/qhd,khd->hqk/dot_general | solution.py:59
  342.5 12.0 %fusion.62 = (f32[]{:T(128)}, f32[1024]{0:T(1024)S(1)}) fusion(f32[1024,4608]{1,0:T(8,128)} %get-tuple-element.296, pred[4608]{0:T(1024)(128)(4,1)S(1)} %get-tuple-element.319, f32[1024]{0:T(1024)S(1)} %get-tuple-element.297), kind=kLoop, calls=%fused_computation.22.clone.1 | loop fusion | flops 23591936 | bytes 18887172 | tf_op jit(solution)/shard_map/while/body/eval_jaxpr/reduce_max | solution.py:69
  354.5 9.0 %fusion.63 = bf16[4,1024,1,128]{3,1,2,0:T(8,128)(2,1)S(1)} fusion(bf16[4,1024,1,128]{3,1,2,0:T(8,128)(2,1)S(1)} %get-tuple-element.309, s32[]{:T(128)} %get-tuple-element.308, bf16[4608,1,128]{2,0,1:T(8,128)(2,1)} %get-tuple-element.322, f32[1024,4608]{1,0:T(8,128)} %get-tuple-element.296, f32[1024]{0:T(1024)S(1)} %get-tuple-element.298, ...), kind=kOutput, calls=%fused_computation.30.clone.1 | convolution fusion | flops 1231683584 | bytes 20329476 | tf_op jit(solution)/shard_map/while/body/eval_jaxpr/hqk,khd->qhd/dot_general | solution.py:66
  364.2 8.8 %fusion.61 = (f32[1024]{0:T(1024)S(1)}, f32[1024,4608]{1,0:T(8,128)}) fusion(pred[4608]{0:T(1024)(128)(4,1)S(1)} %get-tuple-element.319, bf16[4608,1,128]{2,0,1:T(8,128)(2,1)S(1)} %get-tuple-element.321, bf16[4,1024,1,128]{3,1,2,0:T(8,128)(2,1)} %get-tuple-element.320, s32[]{:T(128)} %get-tuple-element.308), kind=kOutput, calls=%fused_computation.23.clone.1 | convolution fusion | flops 1222114304 | bytes 20325376 | tf_op jit(solution)/shard_map/while/body/eval_jaxpr/qhd,khd->hqk/dot_general | solution.py:59
  373.0 12.0 %fusion.62 = (f32[]{:T(128)}, f32[1024]{0:T(1024)S(1)}) fusion(f32[1024,4608]{1,0:T(8,128)} %get-tuple-element.296, pred[4608]{0:T(1024)(128)(4,1)S(1)} %get-tuple-element.319, f32[1024]{0:T(1024)S(1)} %get-tuple-element.297), kind=kLoop, calls=%fused_computation.22.clone.1 | loop fusion | flops 23591936 | bytes 18887172 | tf_op jit(solution)/shard_map/while/body/eval_jaxpr/reduce_max | solution.py:69
  385.0 9.0 %fusion.63 = bf16[4,1024,1,128]{3,1,2,0:T(8,128)(2,1)S(1)} fusion(bf16[4,1024,1,128]{3,1,2,0:T(8,128)(2,1)S(1)} %get-tuple-element.309, s32[]{:T(128)} %get-tuple-element.308, bf16[4608,1,128]{2,0,1:T(8,128)(2,1)} %get-tuple-element.322, f32[1024,4608]{1,0:T(8,128)} %get-tuple-element.296, f32[1024]{0:T(1024)S(1)} %get-tuple-element.298, ...), kind=kOutput, calls=%fused_computation.30.clone.1 | convolution fusion | flops 1231683584 | bytes 20329476 | tf_op jit(solution)/shard_map/while/body/eval_jaxpr/hqk,khd->qhd/dot_general | solution.py:66
  394.8 1.5 pad_maximum_fusion
  396.2 18.4 %copy.38 = bf16[2,4096,1,128]{3,0,2,1:T(2,128)(2,1)} copy(bf16[2,4096,1,128]{3,1,2,0:T(8,128)(2,1)S(1)} %pad_maximum_fusion) | data formatting | bytes 4194304 | tf_op jit(solution)/shard_map/stack | solution.py:78
  414.6 5.3 all-to-all-start.2
  421.2 27.4 %all-to-all-done.2 = bf16[2,4096,1,128]{3,0,2,1:T(2,128)(2,1)S(1)} async-done(((bf16[2,4096,1,128]{3,0,2,1:T(2,128)(2,1)}), bf16[2,4096,1,128]{3,0,2,1:T(2,128)(2,1)S(1)}, u32[]{:S(2)}, u32[]{:S(2)}) %all-to-all-start.2) | async-done | bytes 2097184 | tf_op jit(solution)/shard_map/all_to_all | solution.py:79
  448.9 1.4 copy.40
  450.2 2.3 dot_general.20
  452.6 10.9 %fusion.46 = (f32[2,256]{1,0:T(2,128)S(1)}, f32[2,256,3072]{2,1,0:T(8,128)S(1)}) fusion(bf16[2,256,2048]{2,1,0:T(8,128)(2,1)} %dot_general.20, bf16[2048,3072]{1,0:T(8,128)(2,1)} %all-gather.2.cloned.1.call-done, f32[2,3072]{1,0:T(2,128)S(1)} %get-tuple-element.189, bf16[1,2,256,3072]{3,2,1,0:T(8,128)(2,1)} %param.20), kind=kOutput, calls=%fused_computation.72 | convolution fusion | flops 6448741888 | bytes 24143872 | tf_op jit(solution)/shard_map/dot_general | solution.py:81
  464.3 1.6 fusion.42
  466.0 1.4 maximum_bitcast_fusion
  467.4 36.1 %pmax.7 = f32[1,2]{1,0:T(1,128)} all-reduce(f32[1,2]{1,0:T(1,128)S(1)} %maximum_bitcast_fusion), channel_id=1, replica_groups=mesh['cfg'=2,'req'=4,'seq'=16] {'seq'}, use_global_device_ids=true, to_apply=%region_16.17 | all-reduce | flops 2 | bytes 16 | tf_op jit(solution)/shard_map/pmax | solution.py:108
  504.2 37.3 %psum.7 = f32[2]{0:T(128)S(1)} all-reduce(f32[2]{0:T(128)S(1)} %get-tuple-element.185), channel_id=1, replica_groups=mesh['cfg'=2,'req'=4,'seq'=16] {'seq'}, use_global_device_ids=true, to_apply=%region_13.14 | all-reduce | flops 2 | bytes 16 | tf_op jit(solution)/shard_map/psum | solution.py:107
  (58 shorter events, 15.0 us)
Async XLA Ops:
  7.2 457.1 %copy-start = (bf16[3072,64]{0,1:T(8,128)(2,1)S(1)}, bf16[3072,64]{0,1:T(8,128)(2,1)}, u32[]{:S(2)}) copy-start(bf16[3072,64]{0,1:T(8,128)(2,1)} %param.23) | copy-start | bytes 1179652
  9.4 25.2 %all-to-all-start.1 = ((bf16[2,32,2,16,128]{4,1,2,0,3:T(8,128)(2,1)}), bf16[2,32,2,16,128]{4,1,2,0,3:T(8,128)(2,1)S(1)}, u32[]{:S(2)}, u32[]{:S(2)}) async-start(bf16[2,32,2,16,128]{4,1,2,0,3:T(8,128)(2,1)} %copy.34), calls=%async_computation.1 | async-start | bytes 1048576 | tf_op jit(solution)/shard_map/all_to_all | solution.py:43
  34.6 8.1 %copy-start.6 = (s32[2]{0:T(128)S(1)}, s32[2]{0:T(128)}, u32[]{:S(2)}) copy-start(s32[2]{0:T(128)} %param.16) | copy-start | bytes 28
  34.6 105.1 %all-to-all-start = ((bf16[2,256,3,16,128]{4,1,2,0,3:T(8,128)(2,1)}), bf16[2,256,3,16,128]{4,1,2,0,3:T(8,128)(2,1)}, u32[]{:S(2)}, u32[]{:S(2)}) async-start(bf16[2,256,3,16,128]{4,1,2,0,3:T(8,128)(2,1)} %copy.32), calls=%async_computation | async-start | bytes 12582912 | tf_op jit(solution)/shard_map/all_to_all | solution.py:42
  42.0 410.6 %all-gather.2.cloned.1.call-start = ((), (), s32[]{:S(2)}) async-start(), calls=%async_computation.3 | async-start | bytes 12681216 | tf_op jit(solution)/shard_map/all_gather | solution.py:83
  147.0 122.4 %copy-start.2 = (bf16[512,1,128]{2,0,1:T(8,128)(2,1)S(1)}, bf16[512,1,128]{2,0,1:T(8,128)(2,1)}, u32[]{:S(2)}) copy-start(bf16[512,1,128]{2,0,1:T(8,128)(2,1)} %get-tuple-element.182) | copy-start | bytes 393220
  147.0 122.4 %copy-start.3 = (bf16[512,1,128]{2,0,1:T(8,128)(2,1)S(1)}, bf16[512,1,128]{2,0,1:T(8,128)(2,1)}, u32[]{:S(2)}) copy-start(bf16[512,1,128]{2,0,1:T(8,128)(2,1)} %get-tuple-element.183) | copy-start | bytes 393220
  147.0 125.3 %copy-start.1 = (pred[4608]{0:T(1024)(128)(4,1)S(1)}, pred[4608]{0:T(1024)(128)(4,1)}, u32[]{:S(2)}) copy-start(pred[4608]{0:T(1024)(128)(4,1)} %concatenate.21) | copy-start | bytes 13828
  269.4 2.9 copy-start.9
  394.8 25.2 %copy-start.8 = (s32[2]{0:T(128)S(1)}, s32[2]{0:T(128)}, u32[]{:S(2)}) copy-start(s32[2]{0:T(128)} %param.17) | copy-start | bytes 28
  394.8 25.2 %copy-start.4 = (f32[1,2,3,3072]{3,1,2,0:T(2,128)S(1)}, f32[1,2,3,3072]{3,1,2,0:T(2,128)}, u32[]{:S(2)}) copy-start(f32[1,2,3,3072]{3,1,2,0:T(2,128)} %param.19) | copy-start | bytes 221188
  394.8 25.2 %copy-start.10 = (f32[4]{0:T(128)S(1)}, f32[4]{0:T(128)}, u32[]{:S(2)}) copy-start(f32[4]{0:T(128)} %copy-done.9) | copy-start | bytes 52
  414.6 34.0 %all-to-all-start.2 = ((bf16[2,4096,1,128]{3,0,2,1:T(2,128)(2,1)}), bf16[2,4096,1,128]{3,0,2,1:T(2,128)(2,1)S(1)}, u32[]{:S(2)}, u32[]{:S(2)}) async-start(bf16[2,4096,1,128]{3,0,2,1:T(2,128)(2,1)} %copy.38), calls=%async_computation.2 | async-start | bytes 4194304 | tf_op jit(solution)/shard_map/all_to_all | solution.py:79
  464.3 39.2 %copy-start.5 = (f32[2,256,32]{1,2,0:T(8,128)S(1)}, f32[2,256,32]{1,2,0:T(8,128)}, u32[]{:S(2)}) copy-start(f32[2,256,32]{1,2,0:T(8,128)} %param.21) | copy-start | bytes 196612
  464.3 39.2 %copy-start.7 = (f32[2]{0:T(128)S(1)}, f32[2]{0:T(128)}, u32[]{:S(2)}) copy-start(f32[2]{0:T(128)} %param.18) | copy-start | bytes 28
  465.9 37.5 %collective-permute-start = (f32[2,256,32]{1,2,0:T(8,128)S(1)}, f32[2,256,32]{1,2,0:T(8,128)S(1)}, u32[]{:S(2)}, u32[]{:S(2)}) collective-permute-start(f32[2,256,32]{1,2,0:T(8,128)S(1)} %constant_dynamic-slice_fusion), channel_id=1, source_target_pairs={{0,64},{64,0},{1,65},{65,1},{2,66},{66,2},{3,67},{67,3},{4,68},{68... | collective-permute-start | bytes 196616 | tf_op jit(solution)/shard_map/ppermute | solution.py:15
Sparse Core Ops, SparseCore 0:
  45.9 123.1 all-gather.1
where the time goes:
time: 550 us; the launch traced here: 549 us
  matrix products  154 us (28%)
  waiting for transfers between devices  122 us (22%)
  other arithmetic  109 us (20%)
  blocking collectives  73.4 us (13%)
  local copies, waits for them, and re-layouts  56.1 us (10%)
  starting transfers between devices  20.7 us (4%)
  between operations  14.3 us (3%)
    reduce_max x8, other arithmetic, one_block(): return (mixed_rows, jnp.max(row_max))  97.1 us
    all_to_all x1, waiting for transfers between devices, shards(): lax.all_to_all(joined, 'seq', split_axis=3, concat_axis=1, tiled=True)  93.6 us
    dot_general x8, matrix products, one_block(): jnp.einsum('hqk,khd->qhd', weights, value_rows, preferred_element_type=jn...  74.3 us
    dot_general x8, matrix products, one_block(): jnp.einsum('qhd,khd->hqk', query_rows, key_rows, preferred_element_type=j...  67.2 us
    psum x1, blocking collectives, shards(): total_sq = lax.psum(square_sum, 'seq')  37.3 us
    pmax x1, blocking collectives, shards(): global_max = lax.pmax(local_max, 'seq')  36.1 us
    all_to_all x1, waiting for transfers between devices, shards(): lax.all_to_all(head_rows, 'seq', split_axis=1, concat_axis=2, tiled=True)  27.4 us
    another operation x1, local copies, waits for them, and re-layouts, shards(): head_rows = jnp.stack(mixed_list)  18.4 us
  transfers between devices with their start and end apart: 5, of which 2 were waited for; matrix products, arithmetic and copies ran while one was open for 55% of the time, Pallas kernels for 0%

commit v1 on v0

--- a/solution.py
+++ b/solution.py
@@ -1,3 +1,4 @@
+import functools
 import math
 import jax
 import jax.numpy as jnp
@@ -9,6 +10,25 @@
 STEPS = 4
 time_shift = 1.15
 norm_eps = 1e-06
+
+
+def pass_slabs(x_in, ax_name):
+    n_axis = lax.axis_size(ax_name)
+
+    def pass_wires(later, u_next):
+        if u_next >= n_axis:
+            return later
+        arrivals = []
+        for b in range(n_axis):
+            arrivals.append((b, b ^ u_next))
+        ready = pass_wires(later + lax.ppermute(later, ax_name, perm=arrivals), 2 * u_next)
+        return ready
+
+    all_rows = pass_wires(x_in, 1)
+    return all_rows
+
+
+balance_node_all = functools.partial(pass_slabs, ax_name="seq")
 
 
 def swapped(value, axis, stride):
@@ -104,7 +124,7 @@
     uncond_vel = jnp.where(is_cond, partner, own_part)
     guided = uncond_vel + guidance[:, None, None] * (cond_vel - uncond_vel)
     square_sum = jnp.sum(guided * guided, axis=(1, 2))
-    total_sq = lax.psum(square_sum, "seq")
+    total_sq = balance_node_all(square_sum)
     global_max = lax.pmax(local_max, "seq")
     vel_norm = jnp.sqrt(total_sq / (img_len * half_chan) + norm_eps)
     euler_step = sigma_of(t_index + 1) - sigma_of(t_index)

time: 550 us -> 531 us (0.965)
  blocking collectives: 73.4 us -> 36.1 us
  waiting for transfers between devices: 122 us -> 137 us
    psum x1 -> x0, blocking collectives: 37.3 us -> none  [shards(): total_sq = lax.psum(square_sum, 'seq')]
    ppermute x0 -> x4, waiting for transfers between devices: none -> 15.4 us  [pass_wires(): lax.ppermute(later, ax_name, perm=arrivals)]
  transfers between devices with their start and end apart: 5 -> 9, of which waited for: 2 -> 6; matrix products, arithmetic and copies ran while one was open for 55% -> 57% of each run, Pallas kernels for 0% -> 0%
where the time goes in v1:
time: 531 us; the launch traced here: 529 us
  matrix products  154 us (29%)
  waiting for transfers between devices  137 us (26%)
  other arithmetic  108 us (20%)
  local copies, waits for them, and re-layouts  56 us (11%)
  blocking collectives  36.1 us (7%)
  starting transfers between devices  22.6 us (4%)
  between operations  14.3 us (3%)
    reduce_max x8, other arithmetic, one_block(): return (mixed_rows, jnp.max(row_max))  97.1 us
    all_to_all x1, waiting for transfers between devices, shards(): lax.all_to_all(joined, 'seq', split_axis=3, concat_axis=1, tiled=True)  93.7 us
    dot_general x8, matrix products, one_block(): jnp.einsum('hqk,khd->qhd', weights, value_rows, preferred_element_type=jn...  74.3 us
    dot_general x8, matrix products, one_block(): jnp.einsum('qhd,khd->hqk', query_rows, key_rows, preferred_element_type=j...  67.5 us
    pmax x1, blocking collectives, shards(): global_max = lax.pmax(local_max, 'seq')  36.1 us
    all_to_all x1, waiting for transfers between devices, shards(): lax.all_to_all(head_rows, 'seq', split_axis=1, concat_axis=2, tiled=True)  27.2 us
    another operation x1, local copies, waits for them, and re-layouts, shards(): head_rows = jnp.stack(mixed_list)  18.3 us
    ppermute x4, waiting for transfers between devices, pass_wires(): lax.ppermute(later, ax_name, perm=arrivals)  15.4 us
  transfers between devices with their start and end apart: 9, of which 6 were waited for; matrix products, arithmetic and copies ran while one was open for 57% of the time, Pallas kernels for 0%

profile of v1, /device:TPU:24, one launch (start us, length us, event | category | flops | bytes accessed | tf_op | source)
XLA Modules:
  0.0 529.0 jit_solution(12513004892595249120)
XLA Ops:
  9.4 7.9 %all-to-all-start.1 = ((bf16[2,32,2,16,128]{4,1,2,0,3:T(8,128)(2,1)}), bf16[2,32,2,16,128]{4,1,2,0,3:T(8,128)(2,1)S(1)}, u32[]{:S(2)}, u32[]{:S(2)}) async-start(bf16[2,32,2,16,128]{4,1,2,0,3:T(8,128)(2,1)} %copy.34), calls=%async_computation.1 | async-start | bytes 1048576 | tf_op jit(solution)/shard_map/all_to_all | solution.py:63
  17.3 8.6 %copy.31 = bf16[1,2,256,6144]{2,3,1,0:T(8,128)(2,1)} copy(bf16[1,2,256,6144]{3,2,1,0:T(8,128)(2,1)} %param.14) | data formatting | bytes 12582912 | tf_op args[0]
  25.9 8.6 %copy.32 = bf16[2,256,3,16,128]{4,1,2,0,3:T(8,128)(2,1)} copy(bf16[2,256,3,16,128]{1,4,3,2,0:T(8,128)(2,1)} %bitcast.151) | data formatting | bytes 12582912 | tf_op jit(solution)/shard_map/reshape;squeeze | solution.py:59
  34.6 7.4 %all-to-all-start = ((bf16[2,256,3,16,128]{4,1,2,0,3:T(8,128)(2,1)}), bf16[2,256,3,16,128]{4,1,2,0,3:T(8,128)(2,1)}, u32[]{:S(2)}, u32[]{:S(2)}) async-start(bf16[2,256,3,16,128]{4,1,2,0,3:T(8,128)(2,1)} %copy.32), calls=%async_computation | async-start | bytes 12582912 | tf_op jit(solution)/shard_map/all_to_all | solution.py:62
  46.0 93.7 %all-to-all-done = bf16[2,256,3,16,128]{4,1,2,0,3:T(8,128)(2,1)} async-done(((bf16[2,256,3,16,128]{4,1,2,0,3:T(8,128)(2,1)}), bf16[2,256,3,16,128]{4,1,2,0,3:T(8,128)(2,1)}, u32[]{:S(2)}, u32[]{:S(2)}) %all-to-all-start) | async-done | bytes 6291488 | tf_op jit(solution)/shard_map/all_to_all | solution.py:62
  139.7 3.2 copy.33
  142.9 1.7 slice_bitcast_fusion.2
  146.9 122.6 %while.24 = (s32[]{:T(128)}, bf16[4,1024,1,128]{3,1,2,0:T(8,128)(2,1)}, f32[4]{0:T(128)S(1)}, pred[4608]{0:T(1024)(128)(4,1)S(1)}, bf16[4,1024,1,128]{3,1,2,0:T(...) while((s32[]{:T(128)}, ...), condition=%wide.region_4.5_spmd, body=%wide.region_0.4_spmd.sunk | while | flops 2477389824 | bytes 59542120 | solution.py:91
  146.9 8.2 %fusion.57 = (f32[1024]{0:T(1024)S(1)}, f32[1024,4608]{1,0:T(8,128)}) fusion(pred[4608]{0:T(1024)(128)(4,1)S(1)} %get-tuple-element.343, bf16[4608,1,128]{2,0,1:T(8,128)(2,1)S(1)} %get-tuple-element.345, bf16[4,1024,1,128]{3,1,2,0:T(8,128)(2,1)S(1)} %get-tuple-element.344, s32[]{:T(128)} %get-tuple-element.332), kind=kOutput, calls=%fused_computation.5.clone.1 | convolution fusion | flops 1222114304 | bytes 20325380 | tf_op jit(solution)/shard_map/while/body/eval_jaxpr/qhd,khd->hqk/dot_general | solution.py:79
  155.1 13.3 %fusion.58 = (f32[]{:T(128)}, f32[1024]{0:T(1024)S(1)}) fusion(f32[1024,4608]{1,0:T(8,128)} %get-tuple-element.285, pred[4608]{0:T(1024)(128)(4,1)S(1)} %get-tuple-element.343, f32[1024]{0:T(1024)S(1)} %get-tuple-element.286), kind=kLoop, calls=%fused_computation.4.clone.1 | loop fusion | flops 23591936 | bytes 18887172 | tf_op jit(solution)/shard_map/while/body/eval_jaxpr/reduce_max | solution.py:89
  168.4 9.6 %fusion.59 = bf16[4,1024,1,128]{3,1,2,0:T(8,128)(2,1)} fusion(bf16[4,1024,1,128]{3,1,2,0:T(8,128)(2,1)} %get-tuple-element.333, s32[]{:T(128)} %get-tuple-element.332, bf16[4608,1,128]{2,0,1:T(8,128)(2,1)} %get-tuple-element.346, f32[1024,4608]{1,0:T(8,128)} %get-tuple-element.285, f32[1024]{0:T(1024)S(1)} %get-tuple-element.287, ...), kind=kOutput, calls=%fused_computation.12.clone.1 | convolution fusion | flops 1231683584 | bytes 20329472 | tf_op jit(solution)/shard_map/while/body/eval_jaxpr/hqk,khd->qhd/dot_general | solution.py:86
  178.7 7.9 %fusion.57 = (f32[1024]{0:T(1024)S(1)}, f32[1024,4608]{1,0:T(8,128)}) fusion(pred[4608]{0:T(1024)(128)(4,1)S(1)} %get-tuple-element.343, bf16[4608,1,128]{2,0,1:T(8,128)(2,1)S(1)} %get-tuple-element.345, bf16[4,1024,1,128]{3,1,2,0:T(8,128)(2,1)S(1)} %get-tuple-element.344, s32[]{:T(128)} %get-tuple-element.332), kind=kOutput, calls=%fused_computation.5.clone.1 | convolution fusion | flops 1222114304 | bytes 20325380 | tf_op jit(solution)/shard_map/while/body/eval_jaxpr/qhd,khd->hqk/dot_general | solution.py:79
  186.7 12.0 %fusion.58 = (f32[]{:T(128)}, f32[1024]{0:T(1024)S(1)}) fusion(f32[1024,4608]{1,0:T(8,128)} %get-tuple-element.285, pred[4608]{0:T(1024)(128)(4,1)S(1)} %get-tuple-element.343, f32[1024]{0:T(1024)S(1)} %get-tuple-element.286), kind=kLoop, calls=%fused_computation.4.clone.1 | loop fusion | flops 23591936 | bytes 18887172 | tf_op jit(solution)/shard_map/while/body/eval_jaxpr/reduce_max | solution.py:89
  198.7 9.6 %fusion.59 = bf16[4,1024,1,128]{3,1,2,0:T(8,128)(2,1)} fusion(bf16[4,1024,1,128]{3,1,2,0:T(8,128)(2,1)} %get-tuple-element.333, s32[]{:T(128)} %get-tuple-element.332, bf16[4608,1,128]{2,0,1:T(8,128)(2,1)} %get-tuple-element.346, f32[1024,4608]{1,0:T(8,128)} %get-tuple-element.285, f32[1024]{0:T(1024)S(1)} %get-tuple-element.287, ...), kind=kOutput, calls=%fused_computation.12.clone.1 | convolution fusion | flops 1231683584 | bytes 20329472 | tf_op jit(solution)/shard_map/while/body/eval_jaxpr/hqk,khd->qhd/dot_general | solution.py:86
  209.0 7.9 %fusion.57 = (f32[1024]{0:T(1024)S(1)}, f32[1024,4608]{1,0:T(8,128)}) fusion(pred[4608]{0:T(1024)(128)(4,1)S(1)} %get-tuple-element.343, bf16[4608,1,128]{2,0,1:T(8,128)(2,1)S(1)} %get-tuple-element.345, bf16[4,1024,1,128]{3,1,2,0:T(8,128)(2,1)S(1)} %get-tuple-element.344, s32[]{:T(128)} %get-tuple-element.332), kind=kOutput, calls=%fused_computation.5.clone.1 | convolution fusion | flops 1222114304 | bytes 20325380 | tf_op jit(solution)/shard_map/while/body/eval_jaxpr/qhd,khd->hqk/dot_general | solution.py:79
  216.9 12.0 %fusion.58 = (f32[]{:T(128)}, f32[1024]{0:T(1024)S(1)}) fusion(f32[1024,4608]{1,0:T(8,128)} %get-tuple-element.285, pred[4608]{0:T(1024)(128)(4,1)S(1)} %get-tuple-element.343, f32[1024]{0:T(1024)S(1)} %get-tuple-element.286), kind=kLoop, calls=%fused_computation.4.clone.1 | loop fusion | flops 23591936 | bytes 18887172 | tf_op jit(solution)/shard_map/while/body/eval_jaxpr/reduce_max | solution.py:89
  228.9 9.6 %fusion.59 = bf16[4,1024,1,128]{3,1,2,0:T(8,128)(2,1)} fusion(bf16[4,1024,1,128]{3,1,2,0:T(8,128)(2,1)} %get-tuple-element.333, s32[]{:T(128)} %get-tuple-element.332, bf16[4608,1,128]{2,0,1:T(8,128)(2,1)} %get-tuple-element.346, f32[1024,4608]{1,0:T(8,128)} %get-tuple-element.285, f32[1024]{0:T(1024)S(1)} %get-tuple-element.287, ...), kind=kOutput, calls=%fused_computation.12.clone.1 | convolution fusion | flops 1231683584 | bytes 20329472 | tf_op jit(solution)/shard_map/while/body/eval_jaxpr/hqk,khd->qhd/dot_general | solution.py:86
  239.2 7.9 %fusion.57 = (f32[1024]{0:T(1024)S(1)}, f32[1024,4608]{1,0:T(8,128)}) fusion(pred[4608]{0:T(1024)(128)(4,1)S(1)} %get-tuple-element.343, bf16[4608,1,128]{2,0,1:T(8,128)(2,1)S(1)} %get-tuple-element.345, bf16[4,1024,1,128]{3,1,2,0:T(8,128)(2,1)S(1)} %get-tuple-element.344, s32[]{:T(128)} %get-tuple-element.332), kind=kOutput, calls=%fused_computation.5.clone.1 | convolution fusion | flops 1222114304 | bytes 20325380 | tf_op jit(solution)/shard_map/while/body/eval_jaxpr/qhd,khd->hqk/dot_general | solution.py:79
  247.2 12.0 %fusion.58 = (f32[]{:T(128)}, f32[1024]{0:T(1024)S(1)}) fusion(f32[1024,4608]{1,0:T(8,128)} %get-tuple-element.285, pred[4608]{0:T(1024)(128)(4,1)S(1)} %get-tuple-element.343, f32[1024]{0:T(1024)S(1)} %get-tuple-element.286), kind=kLoop, calls=%fused_computation.4.clone.1 | loop fusion | flops 23591936 | bytes 18887172 | tf_op jit(solution)/shard_map/while/body/eval_jaxpr/reduce_max | solution.py:89
  259.1 9.6 %fusion.59 = bf16[4,1024,1,128]{3,1,2,0:T(8,128)(2,1)} fusion(bf16[4,1024,1,128]{3,1,2,0:T(8,128)(2,1)} %get-tuple-element.333, s32[]{:T(128)} %get-tuple-element.332, bf16[4608,1,128]{2,0,1:T(8,128)(2,1)} %get-tuple-element.346, f32[1024,4608]{1,0:T(8,128)} %get-tuple-element.285, f32[1024]{0:T(1024)S(1)} %get-tuple-element.287, ...), kind=kOutput, calls=%fused_computation.12.clone.1 | convolution fusion | flops 1231683584 | bytes 20329472 | tf_op jit(solution)/shard_map/while/body/eval_jaxpr/hqk,khd->qhd/dot_general | solution.py:86
  269.5 2.7 pad_maximum_fusion.3
  272.4 122.6 %while.25 = (s32[]{:T(128)}, bf16[4,1024,1,128]{3,1,2,0:T(8,128)(2,1)S(1)}, f32[4]{0:T(128)S(1)}, pred[4608]{0:T(1024)(128)(4,1)S(1)}, bf16[4,1024,1,128]{3,1,2,...) while((s32[]{:T(128)}, ...), condition=%wide.region_9.10_spmd, body=%wide.region_5.9_spmd.sunk | while | flops 2477389824 | bytes 59542120 | solution.py:91
  272.6 8.9 %fusion.61 = (f32[1024]{0:T(1024)S(1)}, f32[1024,4608]{1,0:T(8,128)}) fusion(pred[4608]{0:T(1024)(128)(4,1)S(1)} %get-tuple-element.319, bf16[4608,1,128]{2,0,1:T(8,128)(2,1)S(1)} %get-tuple-element.321, bf16[4,1024,1,128]{3,1,2,0:T(8,128)(2,1)} %get-tuple-element.320, s32[]{:T(128)} %get-tuple-element.308), kind=kOutput, calls=%fused_computation.23.clone.1 | convolution fusion | flops 1222114304 | bytes 20325376 | tf_op jit(solution)/shard_map/while/body/eval_jaxpr/qhd,khd->hqk/dot_general | solution.py:79
  281.5 12.0 %fusion.62 = (f32[]{:T(128)}, f32[1024]{0:T(1024)S(1)}) fusion(f32[1024,4608]{1,0:T(8,128)} %get-tuple-element.296, pred[4608]{0:T(1024)(128)(4,1)S(1)} %get-tuple-element.319, f32[1024]{0:T(1024)S(1)} %get-tuple-element.297), kind=kLoop, calls=%fused_computation.22.clone.1 | loop fusion | flops 23591936 | bytes 18887172 | tf_op jit(solution)/shard_map/while/body/eval_jaxpr/reduce_max | solution.py:89
  293.4 9.0 %fusion.63 = bf16[4,1024,1,128]{3,1,2,0:T(8,128)(2,1)S(1)} fusion(bf16[4,1024,1,128]{3,1,2,0:T(8,128)(2,1)S(1)} %get-tuple-element.309, s32[]{:T(128)} %get-tuple-element.308, bf16[4608,1,128]{2,0,1:T(8,128)(2,1)} %get-tuple-element.322, f32[1024,4608]{1,0:T(8,128)} %get-tuple-element.296, f32[1024]{0:T(1024)S(1)} %get-tuple-element.298, ...), kind=kOutput, calls=%fused_computation.30.clone.1 | convolution fusion | flops 1231683584 | bytes 20329476 | tf_op jit(solution)/shard_map/while/body/eval_jaxpr/hqk,khd->qhd/dot_general | solution.py:86
  303.2 8.9 %fusion.61 = (f32[1024]{0:T(1024)S(1)}, f32[1024,4608]{1,0:T(8,128)}) fusion(pred[4608]{0:T(1024)(128)(4,1)S(1)} %get-tuple-element.319, bf16[4608,1,128]{2,0,1:T(8,128)(2,1)S(1)} %get-tuple-element.321, bf16[4,1024,1,128]{3,1,2,0:T(8,128)(2,1)} %get-tuple-element.320, s32[]{:T(128)} %get-tuple-element.308), kind=kOutput, calls=%fused_computation.23.clone.1 | convolution fusion | flops 1222114304 | bytes 20325376 | tf_op jit(solution)/shard_map/while/body/eval_jaxpr/qhd,khd->hqk/dot_general | solution.py:79
  312.1 12.0 %fusion.62 = (f32[]{:T(128)}, f32[1024]{0:T(1024)S(1)}) fusion(f32[1024,4608]{1,0:T(8,128)} %get-tuple-element.296, pred[4608]{0:T(1024)(128)(4,1)S(1)} %get-tuple-element.319, f32[1024]{0:T(1024)S(1)} %get-tuple-element.297), kind=kLoop, calls=%fused_computation.22.clone.1 | loop fusion | flops 23591936 | bytes 18887172 | tf_op jit(solution)/shard_map/while/body/eval_jaxpr/reduce_max | solution.py:89
  324.1 9.0 %fusion.63 = bf16[4,1024,1,128]{3,1,2,0:T(8,128)(2,1)S(1)} fusion(bf16[4,1024,1,128]{3,1,2,0:T(8,128)(2,1)S(1)} %get-tuple-element.309, s32[]{:T(128)} %get-tuple-element.308, bf16[4608,1,128]{2,0,1:T(8,128)(2,1)} %get-tuple-element.322, f32[1024,4608]{1,0:T(8,128)} %get-tuple-element.296, f32[1024]{0:T(1024)S(1)} %get-tuple-element.298, ...), kind=kOutput, calls=%fused_computation.30.clone.1 | convolution fusion | flops 1231683584 | bytes 20329476 | tf_op jit(solution)/shard_map/while/body/eval_jaxpr/hqk,khd->qhd/dot_general | solution.py:86
  333.8 8.9 %fusion.61 = (f32[1024]{0:T(1024)S(1)}, f32[1024,4608]{1,0:T(8,128)}) fusion(pred[4608]{0:T(1024)(128)(4,1)S(1)} %get-tuple-element.319, bf16[4608,1,128]{2,0,1:T(8,128)(2,1)S(1)} %get-tuple-element.321, bf16[4,1024,1,128]{3,1,2,0:T(8,128)(2,1)} %get-tuple-element.320, s32[]{:T(128)} %get-tuple-element.308), kind=kOutput, calls=%fused_computation.23.clone.1 | convolution fusion | flops 1222114304 | bytes 20325376 | tf_op jit(solution)/shard_map/while/body/eval_jaxpr/qhd,khd->hqk/dot_general | solution.py:79
  342.7 12.0 %fusion.62 = (f32[]{:T(128)}, f32[1024]{0:T(1024)S(1)}) fusion(f32[1024,4608]{1,0:T(8,128)} %get-tuple-element.296, pred[4608]{0:T(1024)(128)(4,1)S(1)} %get-tuple-element.319, f32[1024]{0:T(1024)S(1)} %get-tuple-element.297), kind=kLoop, calls=%fused_computation.22.clone.1 | loop fusion | flops 23591936 | bytes 18887172 | tf_op jit(solution)/shard_map/while/body/eval_jaxpr/reduce_max | solution.py:89
  354.7 9.0 %fusion.63 = bf16[4,1024,1,128]{3,1,2,0:T(8,128)(2,1)S(1)} fusion(bf16[4,1024,1,128]{3,1,2,0:T(8,128)(2,1)S(1)} %get-tuple-element.309, s32[]{:T(128)} %get-tuple-element.308, bf16[4608,1,128]{2,0,1:T(8,128)(2,1)} %get-tuple-element.322, f32[1024,4608]{1,0:T(8,128)} %get-tuple-element.296, f32[1024]{0:T(1024)S(1)} %get-tuple-element.298, ...), kind=kOutput, calls=%fused_computation.30.clone.1 | convolution fusion | flops 1231683584 | bytes 20329476 | tf_op jit(solution)/shard_map/while/body/eval_jaxpr/hqk,khd->qhd/dot_general | solution.py:86
  364.4 8.9 %fusion.61 = (f32[1024]{0:T(1024)S(1)}, f32[1024,4608]{1,0:T(8,128)}) fusion(pred[4608]{0:T(1024)(128)(4,1)S(1)} %get-tuple-element.319, bf16[4608,1,128]{2,0,1:T(8,128)(2,1)S(1)} %get-tuple-element.321, bf16[4,1024,1,128]{3,1,2,0:T(8,128)(2,1)} %get-tuple-element.320, s32[]{:T(128)} %get-tuple-element.308), kind=kOutput, calls=%fused_computation.23.clone.1 | convolution fusion | flops 1222114304 | bytes 20325376 | tf_op jit(solution)/shard_map/while/body/eval_jaxpr/qhd,khd->hqk/dot_general | solution.py:79
  373.3 12.0 %fusion.62 = (f32[]{:T(128)}, f32[1024]{0:T(1024)S(1)}) fusion(f32[1024,4608]{1,0:T(8,128)} %get-tuple-element.296, pred[4608]{0:T(1024)(128)(4,1)S(1)} %get-tuple-element.319, f32[1024]{0:T(1024)S(1)} %get-tuple-element.297), kind=kLoop, calls=%fused_computation.22.clone.1 | loop fusion | flops 23591936 | bytes 18887172 | tf_op jit(solution)/shard_map/while/body/eval_jaxpr/reduce_max | solution.py:89
  385.3 9.0 %fusion.63 = bf16[4,1024,1,128]{3,1,2,0:T(8,128)(2,1)S(1)} fusion(bf16[4,1024,1,128]{3,1,2,0:T(8,128)(2,1)S(1)} %get-tuple-element.309, s32[]{:T(128)} %get-tuple-element.308, bf16[4608,1,128]{2,0,1:T(8,128)(2,1)} %get-tuple-element.322, f32[1024,4608]{1,0:T(8,128)} %get-tuple-element.296, f32[1024]{0:T(1024)S(1)} %get-tuple-element.298, ...), kind=kOutput, calls=%fused_computation.30.clone.1 | convolution fusion | flops 1231683584 | bytes 20329476 | tf_op jit(solution)/shard_map/while/body/eval_jaxpr/hqk,khd->qhd/dot_general | solution.py:86
  395.0 1.5 pad_maximum_fusion
  396.5 18.3 %copy.38 = bf16[2,4096,1,128]{3,0,2,1:T(2,128)(2,1)} copy(bf16[2,4096,1,128]{3,1,2,0:T(8,128)(2,1)S(1)} %pad_maximum_fusion) | data formatting | bytes 4194304 | tf_op jit(solution)/shard_map/stack | solution.py:98
  414.8 5.4 %all-to-all-start.2 = ((bf16[2,4096,1,128]{3,0,2,1:T(2,128)(2,1)}), bf16[2,4096,1,128]{3,0,2,1:T(2,128)(2,1)S(1)}, u32[]{:S(2)}, u32[]{:S(2)}) async-start(bf16[2,4096,1,128]{3,0,2,1:T(2,128)(2,1)} %copy.38), calls=%async_computation.2 | async-start | bytes 4194304 | tf_op jit(solution)/shard_map/all_to_all | solution.py:99
  421.5 27.2 %all-to-all-done.2 = bf16[2,4096,1,128]{3,0,2,1:T(2,128)(2,1)S(1)} async-done(((bf16[2,4096,1,128]{3,0,2,1:T(2,128)(2,1)}), bf16[2,4096,1,128]{3,0,2,1:T(2,128)(2,1)S(1)}, u32[]{:S(2)}, u32[]{:S(2)}) %all-to-all-start.2) | async-done | bytes 2097184 | tf_op jit(solution)/shard_map/all_to_all | solution.py:99
  450.4 2.3 dot_general.20
  452.6 10.9 %fusion.46 = (f32[2,256]{1,0:T(2,128)S(1)}, f32[2,256,3072]{2,1,0:T(8,128)S(1)}) fusion(bf16[2,256,2048]{2,1,0:T(8,128)(2,1)} %dot_general.20, bf16[2048,3072]{1,0:T(8,128)(2,1)} %all-gather.2.cloned.1.call-done, f32[2,3072]{1,0:T(2,128)S(1)} %get-tuple-element.189, bf16[1,2,256,3072]{3,2,1,0:T(8,128)(2,1)} %param.20), kind=kOutput, calls=%fused_computation.72 | convolution fusion | flops 6448741888 | bytes 24143872 | tf_op jit(solution)/shard_map/dot_general | solution.py:101
  464.4 1.6 fusion.42
  466.1 1.4 maximum_bitcast_fusion
  467.4 36.1 %pmax.7 = f32[1,2]{1,0:T(1,128)} all-reduce(f32[1,2]{1,0:T(1,128)S(1)} %maximum_bitcast_fusion), channel_id=1, replica_groups=mesh['cfg'=2,'req'=4,'seq'=16] {'seq'}, use_global_device_ids=true, to_apply=%region_15.16 | all-reduce | flops 2 | bytes 16 | tf_op jit(solution)/shard_map/pmax | solution.py:128
  504.3 1.9 collective-permute-start.1
  506.2 1.7 collective-permute-done.1
  507.9 5.1 collective-permute-done.2
  513.0 3.6 collective-permute-done.3
  516.6 5.1 collective-permute-done.4
  (68 shorter events, 19.8 us)
Async XLA Ops:
  7.2 457.2 %copy-start = (bf16[3072,64]{0,1:T(8,128)(2,1)S(1)}, bf16[3072,64]{0,1:T(8,128)(2,1)}, u32[]{:S(2)}) copy-start(bf16[3072,64]{0,1:T(8,128)(2,1)} %param.23) | copy-start | bytes 1179652
  9.4 25.2 %all-to-all-start.1 = ((bf16[2,32,2,16,128]{4,1,2,0,3:T(8,128)(2,1)}), bf16[2,32,2,16,128]{4,1,2,0,3:T(8,128)(2,1)S(1)}, u32[]{:S(2)}, u32[]{:S(2)}) async-start(bf16[2,32,2,16,128]{4,1,2,0,3:T(8,128)(2,1)} %copy.34), calls=%async_computation.1 | async-start | bytes 1048576 | tf_op jit(solution)/shard_map/all_to_all | solution.py:63
  34.5 8.1 %copy-start.6 = (s32[2]{0:T(128)S(1)}, s32[2]{0:T(128)}, u32[]{:S(2)}) copy-start(s32[2]{0:T(128)} %param.16) | copy-start | bytes 28
  34.6 105.1 %all-to-all-start = ((bf16[2,256,3,16,128]{4,1,2,0,3:T(8,128)(2,1)}), bf16[2,256,3,16,128]{4,1,2,0,3:T(8,128)(2,1)}, u32[]{:S(2)}, u32[]{:S(2)}) async-start(bf16[2,256,3,16,128]{4,1,2,0,3:T(8,128)(2,1)} %copy.32), calls=%async_computation | async-start | bytes 12582912 | tf_op jit(solution)/shard_map/all_to_all | solution.py:62
  42.0 410.7 %all-gather.2.cloned.1.call-start = ((), (), s32[]{:S(2)}) async-start(), calls=%async_computation.3 | async-start | bytes 12681216 | tf_op jit(solution)/shard_map/all_gather | solution.py:103
  146.9 122.6 %copy-start.2 = (bf16[512,1,128]{2,0,1:T(8,128)(2,1)S(1)}, bf16[512,1,128]{2,0,1:T(8,128)(2,1)}, u32[]{:S(2)}) copy-start(bf16[512,1,128]{2,0,1:T(8,128)(2,1)} %get-tuple-element.182) | copy-start | bytes 393220
  146.9 122.6 %copy-start.3 = (bf16[512,1,128]{2,0,1:T(8,128)(2,1)S(1)}, bf16[512,1,128]{2,0,1:T(8,128)(2,1)}, u32[]{:S(2)}) copy-start(bf16[512,1,128]{2,0,1:T(8,128)(2,1)} %get-tuple-element.183) | copy-start | bytes 393220
  146.9 125.5 %copy-start.1 = (pred[4608]{0:T(1024)(128)(4,1)S(1)}, pred[4608]{0:T(1024)(128)(4,1)}, u32[]{:S(2)}) copy-start(pred[4608]{0:T(1024)(128)(4,1)} %concatenate.21) | copy-start | bytes 13828
  269.5 2.9 copy-start.9
  395.0 25.2 %copy-start.8 = (s32[2]{0:T(128)S(1)}, s32[2]{0:T(128)}, u32[]{:S(2)}) copy-start(s32[2]{0:T(128)} %param.17) | copy-start | bytes 28
  395.0 25.2 %copy-start.4 = (f32[1,2,3,3072]{3,1,2,0:T(2,128)S(1)}, f32[1,2,3,3072]{3,1,2,0:T(2,128)}, u32[]{:S(2)}) copy-start(f32[1,2,3,3072]{3,1,2,0:T(2,128)} %param.19) | copy-start | bytes 221188
  395.0 25.2 %copy-start.10 = (f32[4]{0:T(128)S(1)}, f32[4]{0:T(128)}, u32[]{:S(2)}) copy-start(f32[4]{0:T(128)} %copy-done.9) | copy-start | bytes 52
  414.8 33.9 %all-to-all-start.2 = ((bf16[2,4096,1,128]{3,0,2,1:T(2,128)(2,1)}), bf16[2,4096,1,128]{3,0,2,1:T(2,128)(2,1)S(1)}, u32[]{:S(2)}, u32[]{:S(2)}) async-start(bf16[2,4096,1,128]{3,0,2,1:T(2,128)(2,1)} %copy.38), calls=%async_computation.2 | async-start | bytes 4194304 | tf_op jit(solution)/shard_map/all_to_all | solution.py:99
  464.3 39.2 %copy-start.5 = (f32[2,256,32]{1,2,0:T(8,128)S(1)}, f32[2,256,32]{1,2,0:T(8,128)}, u32[]{:S(2)}) copy-start(f32[2,256,32]{1,2,0:T(8,128)} %param.21) | copy-start | bytes 196612
  464.4 39.2 %copy-start.7 = (f32[2]{0:T(128)S(1)}, f32[2]{0:T(128)}, u32[]{:S(2)}) copy-start(f32[2]{0:T(128)} %param.18) | copy-start | bytes 28
  466.0 37.5 %collective-permute-start = (f32[2,256,32]{1,2,0:T(8,128)S(1)}, f32[2,256,32]{1,2,0:T(8,128)S(1)}, u32[]{:S(2)}, u32[]{:S(2)}) collective-permute-start(f32[2,256,32]{1,2,0:T(8,128)S(1)} %constant_dynamic-slice_fusion), channel_id=1, source_target_pairs={{0,64},{64,0},{1,65},{65,1},{2,66},{66,2},{3,67},{67,3},{4,68},{68... | collective-permute-start | bytes 196616 | tf_op jit(solution)/shard_map/ppermute | solution.py:35
  504.3 3.6 collective-permute-start.1
  507.9 5.1 collective-permute-start.2
  513.0 3.6 collective-permute-start.3
  516.6 5.1 collective-permute-start.4
Sparse Core Ops, SparseCore 0:
  45.9 123.1 all-gather.1
